TPU v7x, 32 devices: a whole 2x2x4 slice. The times are simulated.
32 devices in a mesh: lat: 16 (over z, y, core), rad: 2 (over x).
Axes of the slice: x: 2, y: 2, z: 4, core: 2. Of those that a mesh axis runs over, the one named last changes fastest.
Arguments:
- displacement: float32 [256, 8, 2048], P('lat', 'rad'), may hold values from -3 to 3
- memory: float32 [256, 8, 2048], P('lat', 'rad'), may hold values from -3 to 3
- ice_class: int32 [256, 2048], P('lat'), may hold values from 0 to 7
- material: int32 [256, 8], P('lat', 'rad'), may hold values from 0 to 7
- mu_table: float32 [8], replicated, may hold values from 0.5 to 4
- decay_table: float32 [8], replicated, may hold values from 0.2 to 0.95
- contrast_table: float32 [8], replicated, may hold values from 0.5 to 2
- gravity_kernel: float32 [256, 8, 8], P('lat', 'rad'), may hold values from -2 to 2
Outputs:
- displacement_out: float32 [256, 8, 2048], P('lat', 'rad')
- memory_out: float32 [256, 8, 2048], P('lat', 'rad')
- potential: float32 [256, 8, 2048], P('lat', 'rad')
All inputs are finite; a program needn't handle non-finite values.
Results may differ from a plain program's by a relative error of at most 0.0028.
Values sent between devices are 32-bit elements; how exact they have to be, the bound alone decides.
A program may use at most 64 MiB of HBM per device.

v0:
```python
import jax
import jax.numpy as jnp
from jax import lax
from jax.sharding import PartitionSpec as P

MODES = 256


load_scale = 0.5
kappa_shift = 0.5
relax_factor = 0.8
coupling = 2.0


def padded_2(x, sides, width):
    for axis, dim in sides:
        devices, length = (lax.axis_size(axis), x.shape[dim])
        up = [(i, (i + 1) % devices) for i in range(devices - 1)]
        down = [(j, i) for i, j in up]
        last = lax.slice_in_dim(x, length - width, length, axis=dim)
        first = lax.slice_in_dim(x, 0, width, axis=dim)
        before = lax.ppermute(last, axis, up)
        after = lax.ppermute(first, axis, down)
        x = jnp.concatenate([before, x, after], axis=dim)
    return x


def lookup(material, table):
    onehot = (
        material[:, :, None] == jnp.arange(table.shape[0], dtype=jnp.int32)[None, None, :]
    ).astype(jnp.float32)
    return jnp.sum(onehot * table[None, None, :], axis=-1)


def fourier_table(nlon, modes):
    longitude = jnp.arange(nlon, dtype=jnp.int32)
    order = jnp.arange(modes, dtype=jnp.int32)
    phase = (longitude[:, None] * order[None, :] % nlon).astype(jnp.float32)
    angle = phase * (2.0 * jnp.pi / nlon)
    scale = jnp.sqrt(jnp.float32(2.0) / nlon)
    return scale * jnp.concatenate([jnp.cos(angle), jnp.sin(angle)], axis=1)


def legendre(cosine, count):

    def step(carry, degree):
        before, current = carry
        nextone = ((2.0 * degree + 1.0) * cosine * current - degree * before) / (degree + 1.0)
        return ((current, nextone), current * jnp.sqrt(degree + 0.5))

    start = (jnp.zeros_like(cosine), jnp.ones_like(cosine))
    _, rows = lax.scan(step, start, jnp.arange(count, dtype=jnp.float32), unroll=16)
    return rows


def sweep(field, memory, source, stiff, decay):
    padded = padded_2(field, (("lat", 0), ("rad", 1)), 1)
    beside = padded[2:, 1:-1] + padded[:-2, 1:-1] + padded[1:-1, 2:] + padded[1:-1, :-2]
    beside = beside + jnp.roll(field, 1, axis=2) + jnp.roll(field, -1, axis=2)
    diagonal = stiff * (6.0 + kappa_shift)
    applied = diagonal * field - stiff * beside
    update = relax_factor * (source - memory - applied) / diagonal
    return (field + update, decay * memory + stiff * update)


def per_device(
    displacement, memory, ice_class, material, mu_table, decay_table, contrast_table, gravity_kernel
):
    lat_dev, r_dev, nlon = displacement.shape
    lat_count = lax.axis_size("lat")
    rad_count = lax.axis_size("rad")
    rad_index = lax.axis_index("rad")
    total_lat = lat_count * lat_dev
    total_rad = rad_count * r_dev
    degrees = gravity_kernel.shape[0] * lat_count
    cols = 2 * MODES
    stiff = lookup(material, mu_table)[:, :, None]
    decay = lookup(material, decay_table)[:, :, None]
    contrast = lookup(material, contrast_table)[:, :, None]
    layer_pos = (rad_index * r_dev + jnp.arange(r_dev, dtype=jnp.int32) + 1).astype(
        jnp.float32
    ) / total_rad
    source = load_scale * ice_class.astype(jnp.float32)[:, None, :] * layer_pos[None, :, None]
    theta_all = (jnp.arange(total_lat, dtype=jnp.float32) + 0.5) * (jnp.pi / total_lat)
    basis_all = legendre(jnp.cos(theta_all), degrees)
    weighted_all = basis_all * (jnp.pi / total_lat * jnp.sin(theta_all))[None, :]
    field, mem = (displacement, memory)
    for step in range(3):
        field, mem = sweep(field, mem, source, stiff, decay)
    rho = contrast * field
    cells = total_lat * total_rad * nlon
    local_mass = jnp.sum(rho)
    mass = lax.psum(local_mass, ("lat", "rad"))
    rho = rho - mass / cells
    table = fourier_table(nlon, MODES)
    spectra = jnp.dot(
        rho.reshape(lat_dev * r_dev, nlon), table, precision=lax.Precision.HIGHEST
    ).reshape(lat_dev, r_dev * cols)
    columns = cols // lat_count
    spread = lax.all_to_all(
        spectra.reshape(lat_dev, r_dev, cols), "lat", split_axis=2, concat_axis=0, tiled=True
    )
    coef_cols = jnp.dot(
        weighted_all, spread.reshape(total_lat, r_dev * columns), precision=lax.Precision.HIGHEST
    ).reshape(degrees, r_dev, columns)
    kernel_every = lax.all_gather(gravity_kernel, "lat", axis=0, tiled=True)
    phi_cols = jnp.einsum(
        "nab,nbk->nak",
        kernel_every,
        lax.all_gather(coef_cols, "rad", axis=1, tiled=True),
        precision=lax.Precision.HIGHEST,
    )
    synth_cols = jnp.dot(
        basis_all.T, phi_cols.reshape(degrees, r_dev * columns), precision=lax.Precision.HIGHEST
    ).reshape(total_lat, r_dev, columns)
    synth = lax.all_to_all(synth_cols, "lat", split_axis=0, concat_axis=2, tiled=True)
    potential = jnp.dot(
        synth.reshape(lat_dev * r_dev, cols), table.T, precision=lax.Precision.HIGHEST
    ).reshape(lat_dev, r_dev, nlon)
    loaded = source + coupling * potential
    for step in range(3):
        field, mem = sweep(field, mem, loaded, stiff, decay)
    return (field, mem, potential)


def solution(mesh):
    placed = (
        P("lat", "rad", None),
        P("lat", "rad", None),
        P("lat", None),
        P("lat", "rad"),
        P(),
        P(),
        P(),
        P("lat", "rad", None),
    )
    return jax.shard_map(
        per_device,
        mesh=mesh,
        in_specs=placed,
        out_specs=(P("lat", "rad", None), P("lat", "rad", None), P("lat", "rad", None)),
        check_vma=False,
    )
```

profile of v0, /device:TPU:10, one launch (start us, length us, event | category | flops | bytes accessed | tf_op | source)
XLA Modules:
  0.0 926.7 jit_solution(2386459225296998901)
XLA Ops:
  10.5 9.1 fusion.17
  19.7 668.2 %while.16 = (s32[]{:T(128)}, f32[256]{0:T(256)S(1)}, f32[256]{0:T(256)S(1)}, f32[16,16,256]{2,1,0:T(8,128)}, f32[16,16]{1,0:T(8,128)S(1)}, /*index=5*/s32[]{:T(128)}, f32[]{:T(128)}, f32[]{:T(128)}, f32[]{:T(128)}, s32[]{:T(128)}) while((s32[]{:T(128)}, f32[256]{0:T(256)S(1)}, f32[256]{0:T(256)S(1)}, ...), condition=%wide.region_3.4_spmd.clone.clone, body=%wide.region_2.0_spmd.clone.clone.sunk | while | flops 26435 | bytes 118772 | solution.py:52
  39.7 9.5 %broadcast_multiply_fusion.27 = (f32[256]{0:T(256)S(1)}, f32[256]{0:T(256)S(1)}, f32[256]{0:T(256)S(1)}, f32[256]{0:T(256)S(1)}, f32[256]{0:T(256)S(1)}, /*index...) fusion(f32[]{:T(128)S(6)} %sqrt.96, ...), kind=kLoop, calls=%fused_computation.22.clone.1 | loop fusion | flops 20480 | bytes 18617 | tf_op jit(solution)/shard_map/while/body/eval_jaxpr/mul | solution.py:49
  81.4 9.5 %broadcast_multiply_fusion.27 = (f32[256]{0:T(256)S(1)}, f32[256]{0:T(256)S(1)}, f32[256]{0:T(256)S(1)}, f32[256]{0:T(256)S(1)}, f32[256]{0:T(256)S(1)}, /*index...) fusion(f32[]{:T(128)S(6)} %sqrt.96, ...), kind=kLoop, calls=%fused_computation.22.clone.1 | loop fusion | flops 20480 | bytes 18617 | tf_op jit(solution)/shard_map/while/body/eval_jaxpr/mul | solution.py:49
  123.2 9.5 %broadcast_multiply_fusion.27 = (f32[256]{0:T(256)S(1)}, f32[256]{0:T(256)S(1)}, f32[256]{0:T(256)S(1)}, f32[256]{0:T(256)S(1)}, f32[256]{0:T(256)S(1)}, /*index...) fusion(f32[]{:T(128)S(6)} %sqrt.96, ...), kind=kLoop, calls=%fused_computation.22.clone.1 | loop fusion | flops 20480 | bytes 18617 | tf_op jit(solution)/shard_map/while/body/eval_jaxpr/mul | solution.py:49
  165.0 9.5 %broadcast_multiply_fusion.27 = (f32[256]{0:T(256)S(1)}, f32[256]{0:T(256)S(1)}, f32[256]{0:T(256)S(1)}, f32[256]{0:T(256)S(1)}, f32[256]{0:T(256)S(1)}, /*index...) fusion(f32[]{:T(128)S(6)} %sqrt.96, ...), kind=kLoop, calls=%fused_computation.22.clone.1 | loop fusion | flops 20480 | bytes 18617 | tf_op jit(solution)/shard_map/while/body/eval_jaxpr/mul | solution.py:49
  206.7 9.5 %broadcast_multiply_fusion.27 = (f32[256]{0:T(256)S(1)}, f32[256]{0:T(256)S(1)}, f32[256]{0:T(256)S(1)}, f32[256]{0:T(256)S(1)}, f32[256]{0:T(256)S(1)}, /*index...) fusion(f32[]{:T(128)S(6)} %sqrt.96, ...), kind=kLoop, calls=%fused_computation.22.clone.1 | loop fusion | flops 20480 | bytes 18617 | tf_op jit(solution)/shard_map/while/body/eval_jaxpr/mul | solution.py:49
  248.5 9.5 %broadcast_multiply_fusion.27 = (f32[256]{0:T(256)S(1)}, f32[256]{0:T(256)S(1)}, f32[256]{0:T(256)S(1)}, f32[256]{0:T(256)S(1)}, f32[256]{0:T(256)S(1)}, /*index...) fusion(f32[]{:T(128)S(6)} %sqrt.96, ...), kind=kLoop, calls=%fused_computation.22.clone.1 | loop fusion | flops 20480 | bytes 18617 | tf_op jit(solution)/shard_map/while/body/eval_jaxpr/mul | solution.py:49
  290.2 9.5 %broadcast_multiply_fusion.27 = (f32[256]{0:T(256)S(1)}, f32[256]{0:T(256)S(1)}, f32[256]{0:T(256)S(1)}, f32[256]{0:T(256)S(1)}, f32[256]{0:T(256)S(1)}, /*index...) fusion(f32[]{:T(128)S(6)} %sqrt.96, ...), kind=kLoop, calls=%fused_computation.22.clone.1 | loop fusion | flops 20480 | bytes 18617 | tf_op jit(solution)/shard_map/while/body/eval_jaxpr/mul | solution.py:49
  332.0 9.5 %broadcast_multiply_fusion.27 = (f32[256]{0:T(256)S(1)}, f32[256]{0:T(256)S(1)}, f32[256]{0:T(256)S(1)}, f32[256]{0:T(256)S(1)}, f32[256]{0:T(256)S(1)}, /*index...) fusion(f32[]{:T(128)S(6)} %sqrt.96, ...), kind=kLoop, calls=%fused_computation.22.clone.1 | loop fusion | flops 20480 | bytes 18617 | tf_op jit(solution)/shard_map/while/body/eval_jaxpr/mul | solution.py:49
  373.8 9.5 %broadcast_multiply_fusion.27 = (f32[256]{0:T(256)S(1)}, f32[256]{0:T(256)S(1)}, f32[256]{0:T(256)S(1)}, f32[256]{0:T(256)S(1)}, f32[256]{0:T(256)S(1)}, /*index...) fusion(f32[]{:T(128)S(6)} %sqrt.96, ...), kind=kLoop, calls=%fused_computation.22.clone.1 | loop fusion | flops 20480 | bytes 18617 | tf_op jit(solution)/shard_map/while/body/eval_jaxpr/mul | solution.py:49
  415.5 9.5 %broadcast_multiply_fusion.27 = (f32[256]{0:T(256)S(1)}, f32[256]{0:T(256)S(1)}, f32[256]{0:T(256)S(1)}, f32[256]{0:T(256)S(1)}, f32[256]{0:T(256)S(1)}, /*index...) fusion(f32[]{:T(128)S(6)} %sqrt.96, ...), kind=kLoop, calls=%fused_computation.22.clone.1 | loop fusion | flops 20480 | bytes 18617 | tf_op jit(solution)/shard_map/while/body/eval_jaxpr/mul | solution.py:49
  457.3 9.5 %broadcast_multiply_fusion.27 = (f32[256]{0:T(256)S(1)}, f32[256]{0:T(256)S(1)}, f32[256]{0:T(256)S(1)}, f32[256]{0:T(256)S(1)}, f32[256]{0:T(256)S(1)}, /*index...) fusion(f32[]{:T(128)S(6)} %sqrt.96, ...), kind=kLoop, calls=%fused_computation.22.clone.1 | loop fusion | flops 20480 | bytes 18617 | tf_op jit(solution)/shard_map/while/body/eval_jaxpr/mul | solution.py:49
  499.1 9.5 %broadcast_multiply_fusion.27 = (f32[256]{0:T(256)S(1)}, f32[256]{0:T(256)S(1)}, f32[256]{0:T(256)S(1)}, f32[256]{0:T(256)S(1)}, f32[256]{0:T(256)S(1)}, /*index...) fusion(f32[]{:T(128)S(6)} %sqrt.96, ...), kind=kLoop, calls=%fused_computation.22.clone.1 | loop fusion | flops 20480 | bytes 18617 | tf_op jit(solution)/shard_map/while/body/eval_jaxpr/mul | solution.py:49
  540.8 9.5 %broadcast_multiply_fusion.27 = (f32[256]{0:T(256)S(1)}, f32[256]{0:T(256)S(1)}, f32[256]{0:T(256)S(1)}, f32[256]{0:T(256)S(1)}, f32[256]{0:T(256)S(1)}, /*index...) fusion(f32[]{:T(128)S(6)} %sqrt.96, ...), kind=kLoop, calls=%fused_computation.22.clone.1 | loop fusion | flops 20480 | bytes 18617 | tf_op jit(solution)/shard_map/while/body/eval_jaxpr/mul | solution.py:49
  582.6 9.5 %broadcast_multiply_fusion.27 = (f32[256]{0:T(256)S(1)}, f32[256]{0:T(256)S(1)}, f32[256]{0:T(256)S(1)}, f32[256]{0:T(256)S(1)}, f32[256]{0:T(256)S(1)}, /*index...) fusion(f32[]{:T(128)S(6)} %sqrt.96, ...), kind=kLoop, calls=%fused_computation.22.clone.1 | loop fusion | flops 20480 | bytes 18617 | tf_op jit(solution)/shard_map/while/body/eval_jaxpr/mul | solution.py:49
  624.4 9.5 %broadcast_multiply_fusion.27 = (f32[256]{0:T(256)S(1)}, f32[256]{0:T(256)S(1)}, f32[256]{0:T(256)S(1)}, f32[256]{0:T(256)S(1)}, f32[256]{0:T(256)S(1)}, /*index...) fusion(f32[]{:T(128)S(6)} %sqrt.96, ...), kind=kLoop, calls=%fused_computation.22.clone.1 | loop fusion | flops 20480 | bytes 18617 | tf_op jit(solution)/shard_map/while/body/eval_jaxpr/mul | solution.py:49
  666.1 9.5 %broadcast_multiply_fusion.27 = (f32[256]{0:T(256)S(1)}, f32[256]{0:T(256)S(1)}, f32[256]{0:T(256)S(1)}, f32[256]{0:T(256)S(1)}, f32[256]{0:T(256)S(1)}, /*index...) fusion(f32[]{:T(128)S(6)} %sqrt.96, ...), kind=kLoop, calls=%fused_computation.22.clone.1 | loop fusion | flops 20480 | bytes 18617 | tf_op jit(solution)/shard_map/while/body/eval_jaxpr/mul | solution.py:49
  697.1 22.2 %all_gather.7 = f32[256,4,8]{2,1,0:T(4,128)} all-gather(f32[16,4,8]{2,1,0:T(4,128)} %copy.96), channel_id=1, replica_groups=mesh['lat'=16,'rad'=2] {'lat'}, dimensions={0}, use_global_device_ids=true | all-gather | bytes 34816 | tf_op jit(solution)/shard_map/all_gather | solution.py:106
  730.1 5.2 collective-permute-start.6
  764.4 40.3 %psum.7 = f32[]{:T(128)} all-reduce(f32[]{:T(128)} %get-tuple-element.179), channel_id=1, replica_groups=mesh['lat'=16,'rad'=2] {'lat','rad'}, use_global_device_ids=true, to_apply=%region_6.7 | all-reduce | flops 1 | bytes 8 | tf_op jit(solution)/shard_map/psum | solution.py:93
  839.6 6.7 all_gather.6
  859.3 5.1 all-to-all-start.1
  876.6 5.7 fusion.5
  (341 shorter events, 194.7 us)
Async XLA Ops:
  2.1 687.7 %collective-permute-start = (f32[1,4,2048]{2,0,1:T(1,128)}, f32[1,4,2048]{2,0,1:T(1,128)}, u32[]{:S(2)}, u32[]{:S(2)}) collective-permute-start(f32[1,4,2048]{2,0,1:T(1,128)} %copy.82), channel_id=1, source_target_pairs={{2,0},{4,2},{6,4},{8,6},{10,8},{12,10},{14,12},{16,14},{18,16},{20... | collective-permute-start | bytes 98312 | tf_op jit(solution)/shard_map/ppermute | solution.py:23
  5.5 684.3 %collective-permute-start.1 = (f32[1,4,2048]{2,0,1:T(1,128)}, f32[1,4,2048]{2,0,1:T(1,128)}, u32[]{:S(2)}, u32[]{:S(2)}) collective-permute-start(f32[1,4,2048]{2,0,1:T(1,128)} %copy.84), channel_id=1, source_target_pairs={{0,2},{2,4},{4,6},{6,8},{8,10},{10,12},{12,14},{14,16},{16,18},{18... | collective-permute-start | bytes 98312 | tf_op jit(solution)/shard_map/ppermute | solution.py:22
  691.3 28.1 %collective-permute-start.2 = (f32[18,1,2048]{2,0,1:T(8,128)}, f32[18,1,2048]{2,0,1:T(8,128)}, u32[]{:S(2)}, u32[]{:S(2)}) collective-permute-start(f32[18,1,2048]{2,0,1:T(8,128)} %get-tuple-element.227), channel_id=1, source_target_pairs={{1,0},{3,2},{5,4},{7,6},{9,8},{11,10},{13,12},{15,14},{17,16},{19,... | collective-permute-start | bytes 442376 | tf_op jit(solution)/shard_map/ppermute | solution.py:23
  694.4 24.9 %collective-permute-start.3 = (f32[18,1,2048]{2,0,1:T(8,128)}, f32[18,1,2048]{2,0,1:T(8,128)}, u32[]{:S(2)}, u32[]{:S(2)}) collective-permute-start(f32[18,1,2048]{2,0,1:T(8,128)} %get-tuple-element.228), channel_id=1, source_target_pairs={{0,1},{2,3},{4,5},{6,7},{8,9},{10,11},{12,13},{14,15},{16,17},{18,... | collective-permute-start | bytes 442376 | tf_op jit(solution)/shard_map/ppermute | solution.py:22
  723.9 6.1 collective-permute-start.5
  730.1 8.4 collective-permute-start.6
  735.4 7.6 collective-permute-start.7
  743.8 4.5 collective-permute-start.8
  745.7 7.3 collective-permute-start.9
  753.1 4.6 collective-permute-start.10
  754.5 7.6 collective-permute-start.11
  816.0 10.7 %all-to-all-start = ((f32[16,1,2048]{2,1,0:T(1,128)}), f32[16,1,2048]{2,1,0:T(1,128)}, u32[]{:S(2)}, u32[]{:S(2)}) async-start(f32[16,1,2048]{2,1,0:T(1,128)} %reshape.112), calls=%async_computation | async-start | bytes 262144 | tf_op jit(solution)/shard_map/all_to_all | solution.py:100
  820.3 44.8 %collective-permute-start.12 = (f32[1,4,2048]{2,0,1:T(1,128)}, f32[1,4,2048]{2,0,1:T(1,128)}, u32[]{:S(2)}, u32[]{:S(2)}) collective-permute-start(f32[1,4,2048]{2,0,1:T(1,128)} %get-tuple-element.242), channel_id=1, source_target_pairs={{2,0},{4,2},{6,4},{8,6},{10,8},{12,10},{14,12},{16,14},{18,16},{20... | collective-permute-start | bytes 98312 | tf_op jit(solution)/shard_map/ppermute | solution.py:23
  823.4 41.7 %collective-permute-start.13 = (f32[1,4,2048]{2,0,1:T(1,128)}, f32[1,4,2048]{2,0,1:T(1,128)}, u32[]{:S(2)}, u32[]{:S(2)}) collective-permute-start(f32[1,4,2048]{2,0,1:T(1,128)} %get-tuple-element.241), channel_id=1, source_target_pairs={{0,2},{2,4},{4,6},{6,8},{8,10},{10,12},{12,14},{14,16},{16,18},{18... | collective-permute-start | bytes 98312 | tf_op jit(solution)/shard_map/ppermute | solution.py:22
  859.3 12.0 %all-to-all-start.1 = ((f32[16,1,2048]{2,1,0:T(1,128)}), f32[16,1,2048]{2,1,0:T(1,128)S(1)}, u32[]{:S(2)}, u32[]{:S(2)}) async-start(f32[16,1,2048]{2,1,0:T(1,128)} %reshape.114), calls=%async_computation.1 | async-start | bytes 262144 | tf_op jit(solution)/shard_map/all_to_all | solution.py:116
  866.7 15.6 %collective-permute-start.14 = (f32[18,1,2048]{2,0,1:T(8,128)}, f32[18,1,2048]{2,0,1:T(8,128)}, u32[]{:S(2)}, u32[]{:S(2)}) collective-permute-start(f32[18,1,2048]{2,0,1:T(8,128)} %get-tuple-element.221), channel_id=1, source_target_pairs={{1,0},{3,2},{5,4},{7,6},{9,8},{11,10},{13,12},{15,14},{17,16},{19,... | collective-permute-start | bytes 442376 | tf_op jit(solution)/shard_map/ppermute | solution.py:23
  870.0 12.3 %collective-permute-start.15 = (f32[18,1,2048]{2,0,1:T(8,128)}, f32[18,1,2048]{2,0,1:T(8,128)}, u32[]{:S(2)}, u32[]{:S(2)}) collective-permute-start(f32[18,1,2048]{2,0,1:T(8,128)} %get-tuple-element.222), channel_id=1, source_target_pairs={{0,1},{2,3},{4,5},{6,7},{8,9},{10,11},{12,13},{14,15},{16,17},{18,... | collective-permute-start | bytes 442376 | tf_op jit(solution)/shard_map/ppermute | solution.py:22
  884.4 6.1 collective-permute-start.16
  887.2 6.1 collective-permute-start.17
  893.4 8.1 collective-permute-start.18
  898.3 7.6 collective-permute-start.19
  908.5 6.1 collective-permute-start.21
  914.7 4.6 collective-permute-start.22
  916.2 7.6 collective-permute-start.23
  (17 other events, 1542.8 us)
where the time goes:
time: 937 us; the launch traced here: 927 us
  loops' own time  484 us (52%)
  other arithmetic  188 us (20%)
  blocking collectives  69.3 us (7%)
  starting transfers between devices  64.2 us (7%)
  local copies, waits for them, and re-layouts  61.7 us (7%)
  waiting for transfers between devices  39.4 us (4%)
  matrix products  17.9 us (2%)
    another operation x1, loops' own time, legendre(): lax.scan(step, start, jnp.arange(count, dtype=jnp.float32), unroll=16)  484 us
    mul x144, other arithmetic, step(): return ((current, nextone), current * jnp.sqrt(degree + 0.5))  162 us
    psum x1, blocking collectives, per_device(): mass = lax.psum(local_mass, ('lat', 'rad'))  40.3 us
    ppermute x12, starting transfers between devices, padded_2(): after = lax.ppermute(first, axis, down)  34 us
    ppermute x12, waiting for transfers between devices, padded_2(): before = lax.ppermute(last, axis, up)  32.2 us
    all_gather x1, blocking collectives, per_device(): kernel_every = lax.all_gather(gravity_kernel, 'lat', axis=0, tiled=True)  22.2 us
    ppermute x12, starting transfers between devices, padded_2(): before = lax.ppermute(last, axis, up)  20.8 us
  transfers between devices with their start and end apart: 26, of which 12 were waited for; matrix products, arithmetic and copies ran while one was open for 26% of the time, Pallas kernels for 0%

commit v1 on v0

v1 whole, which is shorter than its diff:
```python
import jax
import jax.numpy as jnp
import numpy as np
from jax import lax
from jax.sharding import PartitionSpec as P

MODES = 256


load_scale = 0.5
kappa_shift = 0.5
relax_factor = 0.8
coupling = 2.0
HIGH = lax.Precision.HIGH


def lookup(material, table):
    onehot = (
        material[:, :, None] == jnp.arange(table.shape[0], dtype=jnp.int32)[None, None, :]
    ).astype(jnp.float32)
    return jnp.sum(onehot * table[None, None, :], axis=-1)


def fourier_parts(nlon, modes, minor=128):
    order = np.arange(modes)
    parts = []
    for place in (np.arange(nlon // minor) * minor, np.arange(minor)):
        angle = (place[:, None] * order[None, :] % nlon) * (2.0 * np.pi / nlon)
        parts += [np.cos(angle), np.sin(angle)]
    scale = np.sqrt(2.0 / nlon)
    return [(part * f).astype(np.float32) for part, f in zip(parts, (scale, scale, 1.0, 1.0))]


def fourier_table(nlon, modes):
    ca, sa, cb, sb = lax.optimization_barrier([jnp.asarray(p) for p in fourier_parts(nlon, modes)])
    ca, sa, cb, sb = ca[:, None], sa[:, None], cb[None], sb[None]
    cos = (ca * cb - sa * sb).reshape(nlon, modes)
    sin = (sa * cb + ca * sb).reshape(nlon, modes)
    return jnp.concatenate([cos, sin], axis=1)


def legendre(lat, degrees):
    theta = np.pi * (np.arange(lat) + 0.5) / lat
    cosine = np.cos(theta)
    before, current, rows = np.zeros(lat), np.ones(lat), []
    for n in range(degrees):
        rows.append(current * np.sqrt(n + 0.5))
        before, current = current, ((2.0 * n + 1.0) * cosine * current - n * before) / (n + 1.0)
    basis = np.stack(rows)
    weighted = basis * (np.pi / lat * np.sin(theta))[None, :]
    return basis, weighted


def neighbours(x, axis, dim):
    devices, length = (lax.axis_size(axis), x.shape[dim])
    up = [(i, i + 1) for i in range(devices - 1)]
    down = [(j, i) for i, j in up]
    last = lax.slice_in_dim(x, length - 1, length, axis=dim)
    first = lax.slice_in_dim(x, 0, 1, axis=dim)
    return lax.ppermute(last, axis, up), lax.ppermute(first, axis, down)


def sweep(field, memory, source, stiff, decay):
    beside = jnp.roll(field, 1, axis=2) + jnp.roll(field, -1, axis=2)
    for axis, dim in (("lat", 0), ("rad", 1)):
        length = field.shape[dim]
        before, after = neighbours(field, axis, dim)
        beside = beside + jnp.concatenate(
            [before, lax.slice_in_dim(field, 0, length - 1, axis=dim)], axis=dim
        )
        beside = beside + jnp.concatenate(
            [lax.slice_in_dim(field, 1, length, axis=dim), after], axis=dim
        )
    diagonal = 6.0 + kappa_shift
    update = relax_factor * (
        (source - memory) * (1.0 / (stiff * diagonal)) - field + beside * (1.0 / diagonal)
    )
    return (field + update, decay * memory + stiff * update)


def per_device(
    displacement, memory, ice_class, material, mu_table, decay_table, contrast_table, gravity_kernel
):
    lat_dev, r_dev, nlon = displacement.shape
    lat_count = lax.axis_size("lat")
    rad_count = lax.axis_size("rad")
    rad_index = lax.axis_index("rad")
    total_lat = lat_count * lat_dev
    total_rad = rad_count * r_dev
    degrees = gravity_kernel.shape[0] * lat_count
    cols = 2 * MODES
    columns = cols // lat_count
    kernel_every = lax.all_gather(gravity_kernel, "lat", axis=0, tiled=True)
    stiff = lookup(material, mu_table)[:, :, None]
    decay = lookup(material, decay_table)[:, :, None]
    contrast = lookup(material, contrast_table)[:, :, None]
    layer_pos = (rad_index * r_dev + jnp.arange(r_dev, dtype=jnp.int32) + 1).astype(
        jnp.float32
    ) / total_rad
    source = load_scale * ice_class.astype(jnp.float32)[:, None, :] * layer_pos[None, :, None]
    basis, weighted = legendre(total_lat, degrees)
    projection = jnp.asarray(
        np.concatenate([weighted, np.ones((8, total_lat))]).astype(np.float32)
    )
    weight_sum = jnp.asarray(weighted.sum(axis=1).astype(np.float32))
    basis = jnp.asarray(basis.T.astype(np.float32))
    table = fourier_table(nlon, MODES)
    field, mem = (displacement, memory)
    for step in range(3):
        field, mem = sweep(field, mem, source, stiff, decay)
    rho = contrast * field
    spectra = jnp.dot(rho.reshape(lat_dev * r_dev, nlon), table, precision=HIGH)
    spread = lax.all_to_all(
        spectra.reshape(lat_dev, r_dev, cols), "lat", split_axis=2, concat_axis=0, tiled=True
    )
    coef_cols = jnp.dot(
        projection, spread.reshape(total_lat, r_dev * columns), precision=HIGH
    ).reshape(degrees + 8, r_dev, columns)
    coef_all = lax.all_gather(coef_cols, "rad", axis=1, tiled=True)
    first_order = (lax.axis_index("lat") * columns + jnp.arange(columns, dtype=jnp.int32)) == 0
    mean_row = jnp.sum(coef_all[degrees], axis=0) / (total_lat * total_rad)
    mean_row = jnp.where(first_order, mean_row, 0.0)
    coef_all = coef_all[:degrees] - weight_sum[:, None, None] * mean_row[None, None, :]
    phi_cols = jnp.sum(kernel_every[:, :, :, None] * coef_all[:, None, :, :], axis=2)
    synth_cols = jnp.dot(
        basis, phi_cols.reshape(degrees, r_dev * columns), precision=HIGH
    ).reshape(total_lat, r_dev, columns)
    synth = lax.all_to_all(synth_cols, "lat", split_axis=0, concat_axis=2, tiled=True)
    potential = lax.dot_general(
        synth.reshape(lat_dev * r_dev, cols), table, (((1,), (1,)), ((), ())), precision=HIGH
    ).reshape(lat_dev, r_dev, nlon)
    loaded = source + coupling * potential
    for step in range(3):
        field, mem = sweep(field, mem, loaded, stiff, decay)
    return (field, mem, potential)


def solution(mesh):
    placed = (
        P("lat", "rad", None),
        P("lat", "rad", None),
        P("lat", None),
        P("lat", "rad"),
        P(),
        P(),
        P(),
        P("lat", "rad", None),
    )
    return jax.shard_map(
        per_device,
        mesh=mesh,
        in_specs=placed,
        out_specs=(P("lat", "rad", None), P("lat", "rad", None), P("lat", "rad", None)),
        check_vma=False,
    )
```

time: 937 us -> 197 us (0.21)
  loops' own time: 484 us -> 0 us
  other arithmetic: 188 us -> 13.1 us
  blocking collectives: 69.3 us -> 28.9 us
  waiting for transfers between devices: 39.4 us -> 9.54 us
  starting transfers between devices: 64.2 us -> 85.5 us
  local copies, waits for them, and re-layouts: 61.7 us -> 48.3 us
  matrix products: 17.9 us -> 7.01 us
    another operation x1 -> x0, loops' own time: 484 us -> none  [legendre(): lax.scan(step, start, jnp.arange(count, dtype=jnp.float32), unroll=16)]
    mul x147 -> x2, other arithmetic: 163 us -> 0.08 us  [the longest x1 0.07 us: per_device(): weight_sum[:, None, None] * mean_row[None, None, :]]
    psum x1 -> x0, blocking collectives: 40.3 us -> none  [per_device(): mass = lax.psum(local_mass, ('lat', 'rad'))]
    ppermute x24, waiting for transfers between devices: 39.4 us -> 4.9 us  [neighbours(): return (lax.ppermute(last, axis, up), lax.ppermute(first, axis, down))]
    ppermute x24, starting transfers between devices: 54.8 us -> 76.4 us  [neighbours(): return (lax.ppermute(last, axis, up), lax.ppermute(first, axis, down))]
    dot_general x5 -> x4, matrix products: 17.9 us -> 7.01 us  [the longest x1 3.78 us: per_device(): lax.dot_general(synth.reshape(lat_dev * r_dev, cols), table, (((1,), (1,)...]
    dynamic_update_slice x16 -> x0, local copies, waits for them, and re-layouts: 9.66 us -> none  [legendre(): lax.scan(step, start, jnp.arange(count, dtype=jnp.float32), unroll=16)]
    unnamed x39 -> x82, local copies, waits for them, and re-layouts: 14.6 us -> 21.2 us
  transfers between devices with their start and end apart: 26 -> 26, of which waited for: 12 -> 5; matrix products, arithmetic and copies ran while one was open for 26% -> 17% of each run, Pallas kernels for 0% -> 0%
where the time goes in v1:
time: 197 us; the launch traced here: 194 us
  starting transfers between devices  85.5 us (43%)
  local copies, waits for them, and re-layouts  48.3 us (25%)
  blocking collectives  28.9 us (15%)
  other arithmetic  13.1 us (7%)
  waiting for transfers between devices  9.54 us (5%)
  matrix products  7.01 us (4%)
    ppermute x24, starting transfers between devices, neighbours(): return (lax.ppermute(last, axis, up), lax.ppermute(first, axis, down))  76.4 us
    unnamed x82, local copies, waits for them, and re-layouts  21.2 us
    all_gather x1, blocking collectives, per_device(): kernel_every = lax.all_gather(gravity_kernel, 'lat', axis=0, tiled=True)  20.8 us
    add x7, other arithmetic, sweep(): return (field + update, decay * memory + stiff * update)  8.58 us
    all_gather x1, blocking collectives, per_device(): coef_all = lax.all_gather(coef_cols, 'rad', axis=1, tiled=True)  8.12 us
    slice x12, local copies, waits for them, and re-layouts, sweep(): beside = jnp.roll(field, 1, axis=2) + jnp.roll(field, -1, axis=2)  5.32 us
    slice x12, local copies, waits for them, and re-layouts, sweep(): lax.slice_in_dim(field, 0, length - 1, axis=dim)  4.96 us
    ppermute x24, waiting for transfers between devices, neighbours(): return (lax.ppermute(last, axis, up), lax.ppermute(first, axis, down))  4.9 us
  transfers between devices with their start and end apart: 26, of which 5 were waited for; matrix products, arithmetic and copies ran while one was open for 17% of the time, Pallas kernels for 0%

profile of v1, /device:TPU:10, one launch (start us, length us, event | category | flops | bytes accessed | tf_op | source)
XLA Modules:
  0.0 193.9 jit_solution(3203658497385336375)
XLA Ops:
  4.2 5.9 %collective-permute-start.3 = (f32[16,1,2048]{2,0,1:T(8,128)}, f32[16,1,2048]{2,0,1:T(8,128)}, u32[]{:S(2)}, u32[]{:S(2)}) collective-permute-start(f32[16,1,2048]{2,0,1:T(8,128)} %copy.140), channel_id=1, source_target_pairs={{1,0},{3,2},{5,4},{7,6},{9,8},{11,10},{13,12},{15,14},{17,16},{19,... | collective-permute-start | bytes 393224 | tf_op jit(solution)/shard_map/ppermute | solution.py:60
  14.1 4.5 %collective-permute-start.1 = (f32[1,4,2048]{2,0,1:T(1,128)}, f32[1,4,2048]{2,0,1:T(1,128)}, u32[]{:S(2)}, u32[]{:S(2)}) collective-permute-start(f32[1,4,2048]{2,0,1:T(1,128)} %copy.103), channel_id=1, source_target_pairs={{2,0},{4,2},{6,4},{8,6},{10,8},{12,10},{14,12},{16,14},{18,16},{20... | collective-permute-start | bytes 98312 | tf_op jit(solution)/shard_map/ppermute | solution.py:60
  18.6 2.3 %fusion.85 = (f32[16,4,2047]{2,1,0:T(4,128)}, f32[16,4,2047]{2,1,0:T(4,128)S(1)}) fusion(f32[16,4,2048]{2,1,0:T(4,128)} %param.15), kind=kLoop, calls=%fused_computation.117 | loop fusion | bytes 2096128 | tf_op jit(solution)/shard_map/jit(_roll_static)/slice | solution.py:64
  26.2 2.2 %copy.132 = f32[16,4,2047]{2,0,1:T(8,128)} copy(f32[16,4,2047]{2,1,0:T(4,128)} %get-tuple-element.101) | data formatting | bytes 1048064
  31.7 2.1 %copy.138 = f32[16,3,2048]{2,0,1:T(8,128)} copy(f32[16,3,2048]{2,1,0:T(4,128)} %get-tuple-element.109) | data formatting | bytes 786432
  35.5 20.8 %all_gather.6 = f32[256,4,8]{2,1,0:T(4,128)} all-gather(f32[16,4,8]{2,1,0:T(4,128)S(1)} %copy.110), channel_id=1, replica_groups=mesh['lat'=16,'rad'=2] {'lat'}, dimensions={0}, use_global_device_ids=true | all-gather | bytes 34816 | tf_op jit(solution)/shard_map/all_gather | solution.py:93
  58.1 2.8 %multiply_add_fusion.13 = (f32[16,4,2048]{2,0,1:T(8,128)S(1)}, f32[16,4,2048]{2,0,1:T(8,128)S(1)}) fusion(f32[16,4,2048]{2,1,0:T(4,128)S(1)} %copy-done, f32[16,1,2048]{2,0,1:T(8,128)} %collective-permute-done.3, f32[16,3,2048]{2,0,1:T(8,128)} %copy.141, f32[16,3,2048]{2,0,1:T(8,128)} %copy.138, f32[16,1,2048]{2,0,1:T(8,128)} %collective-permute-done.2, ...), kind=kLoop, calls=%fused_computation.70 | loop fusion | flops 2490368 | bytes 5374224 | tf_op jit(solution)/shard_map/add | solution.py:78
  62.7 4.6 %collective-permute-start.7 = (f32[16,1,2048]{2,0,1:T(8,128)S(1)}, f32[16,1,2048]{2,0,1:T(8,128)S(1)}, u32[]{:S(2)}, u32[]{:S(2)}) collective-permute-start(f32[16,1,2048]{2,0,1:T(8,128)S(1)} %get-tuple-element.96), channel_id=1, source_target_pairs={{1,0},{3,2},{5,4},{7,6},{9,8},{11,10},{13,12},{15,14},{17,16},{19,... | collective-permute-start | bytes 393224 | tf_op jit(solution)/shard_map/ppermute | solution.py:60
  69.2 4.5 %collective-permute-start.5 = (f32[1,4,2048]{2,0,1:T(1,128)S(1)}, f32[1,4,2048]{2,0,1:T(1,128)S(1)}, u32[]{:S(2)}, u32[]{:S(2)}) collective-permute-start(f32[1,4,2048]{2,0,1:T(1,128)S(1)} %get-tuple-element.92), channel_id=1, source_target_pairs={{2,0},{4,2},{6,4},{8,6},{10,8},{12,10},{14,12},{16,14},{18,16},{20... | collective-permute-start | bytes 98312 | tf_op jit(solution)/shard_map/ppermute | solution.py:60
  77.9 4.6 %collective-permute-start.11 = (f32[16,1,2048]{2,0,1:T(8,128)S(1)}, f32[16,1,2048]{2,0,1:T(8,128)S(1)}, u32[]{:S(2)}, u32[]{:S(2)}) collective-permute-start(f32[16,1,2048]{2,0,1:T(8,128)S(1)} %get-tuple-element.84), channel_id=1, source_target_pairs={{1,0},{3,2},{5,4},{7,6},{9,8},{11,10},{13,12},{15,14},{17,16},{19,... | collective-permute-start | bytes 393224 | tf_op jit(solution)/shard_map/ppermute | solution.py:60
  84.4 4.5 %collective-permute-start.9 = (f32[1,4,2048]{2,0,1:T(1,128)S(1)}, f32[1,4,2048]{2,0,1:T(1,128)S(1)}, u32[]{:S(2)}, u32[]{:S(2)}) collective-permute-start(f32[1,4,2048]{2,0,1:T(1,128)S(1)} %get-tuple-element.80), channel_id=1, source_target_pairs={{2,0},{4,2},{6,4},{8,6},{10,8},{12,10},{14,12},{16,14},{18,16},{20... | collective-permute-start | bytes 98312 | tf_op jit(solution)/shard_map/ppermute | solution.py:60
  98.2 2.7 %reshape.115 = f32[16,1,2048]{2,1,0:T(1,128)} reshape(f32[512,4,16]{2,1,0:T(4,128)} %bitcast.29) | data formatting | bytes 262144
  100.9 4.5 %all-to-all-start = ((f32[16,1,2048]{2,1,0:T(1,128)}), f32[16,1,2048]{2,1,0:T(1,128)S(1)}, u32[]{:S(2)}, u32[]{:S(2)}) async-start(f32[16,1,2048]{2,1,0:T(1,128)} %reshape.115), calls=%async_computation | async-start | bytes 262144 | tf_op jit(solution)/shard_map/all_to_all | solution.py:113
  106.2 4.6 %all-to-all-done = f32[16,1,2048]{2,1,0:T(1,128)S(1)} async-done(((f32[16,1,2048]{2,1,0:T(1,128)}), f32[16,1,2048]{2,1,0:T(1,128)S(1)}, u32[]{:S(2)}, u32[]{:S(2)}) %all-to-all-start) | async-done | bytes 131104 | tf_op jit(solution)/shard_map/all_to_all | solution.py:113
  113.9 2.4 %copy.113 = f32[16,4,16,32]{3,1,0,2:T(4,128)} copy(f32[16,4,16,32]{0,1,3,2:T(4,128)} %bitcast.30) | data formatting | bytes 262144 | tf_op jit(solution)/shard_map/all_to_all | solution.py:113
  118.9 8.1 %all_gather.7 = f32[264,8,32]{0,2,1:T(8,128)S(1)} all-gather(f32[264,4,32]{0,2,1:T(8,128)S(1)} %bitcast.33), channel_id=1, replica_groups=mesh['lat'=16,'rad'=2] {'rad'}, dimensions={1}, use_global_device_ids=true | all-gather | bytes 405504 | tf_op jit(solution)/shard_map/all_gather | solution.py:119
  130.7 4.6 %all-to-all-start.1 = ((f32[16,1,2048]{2,1,0:T(1,128)}), f32[16,1,2048]{2,1,0:T(1,128)S(1)}, u32[]{:S(2)}, u32[]{:S(2)}) async-start(f32[16,1,2048]{2,1,0:T(1,128)} %reshape.117), calls=%async_computation.1 | async-start | bytes 262144 | tf_op jit(solution)/shard_map/all_to_all | solution.py:128
  137.3 5.9 %collective-permute-start.15 = (f32[16,1,2048]{2,0,1:T(8,128)}, f32[16,1,2048]{2,0,1:T(8,128)}, u32[]{:S(2)}, u32[]{:S(2)}) collective-permute-start(f32[16,1,2048]{2,0,1:T(8,128)} %get-tuple-element.72), channel_id=1, source_target_pairs={{1,0},{3,2},{5,4},{7,6},{9,8},{11,10},{13,12},{15,14},{17,16},{19,... | collective-permute-start | bytes 393224 | tf_op jit(solution)/shard_map/ppermute | solution.py:60
  145.1 4.5 %collective-permute-start.13 = (f32[1,4,2048]{2,0,1:T(1,128)}, f32[1,4,2048]{2,0,1:T(1,128)}, u32[]{:S(2)}, u32[]{:S(2)}) collective-permute-start(f32[1,4,2048]{2,0,1:T(1,128)} %get-tuple-element.68), channel_id=1, source_target_pairs={{2,0},{4,2},{6,4},{8,6},{10,8},{12,10},{14,12},{16,14},{18,16},{20... | collective-permute-start | bytes 98312 | tf_op jit(solution)/shard_map/ppermute | solution.py:60
  155.6 3.8 %fusion = f32[16,4,2048]{2,0,1:T(8,128)S(1)} fusion(f32[16,4,512]{2,0,1:T(8,128)S(1)} %dot_general.23, f32[2048,256]{1,0:T(8,128)} %bitcast.27, f32[2048,256]{1,0:T(8,128)S(1)} %bitcast.26), kind=kOutput, calls=%fused_computation.1 | convolution fusion | flops 403701760 | bytes 4849664 | tf_op jit(solution)/shard_map/dot_general | solution.py:129
  163.1 4.6 %collective-permute-start.19 = (f32[16,1,2048]{2,0,1:T(8,128)S(1)}, f32[16,1,2048]{2,0,1:T(8,128)S(1)}, u32[]{:S(2)}, u32[]{:S(2)}) collective-permute-start(f32[16,1,2048]{2,0,1:T(8,128)S(1)} %get-tuple-element.60), channel_id=1, source_target_pairs={{1,0},{3,2},{5,4},{7,6},{9,8},{11,10},{13,12},{15,14},{17,16},{19,... | collective-permute-start | bytes 393224 | tf_op jit(solution)/shard_map/ppermute | solution.py:60
  169.6 4.5 %collective-permute-start.17 = (f32[1,4,2048]{2,0,1:T(1,128)S(1)}, f32[1,4,2048]{2,0,1:T(1,128)S(1)}, u32[]{:S(2)}, u32[]{:S(2)}) collective-permute-start(f32[1,4,2048]{2,0,1:T(1,128)S(1)} %get-tuple-element.56), channel_id=1, source_target_pairs={{2,0},{4,2},{6,4},{8,6},{10,8},{12,10},{14,12},{16,14},{18,16},{20... | collective-permute-start | bytes 98312 | tf_op jit(solution)/shard_map/ppermute | solution.py:60
  178.2 4.6 %collective-permute-start.23 = (f32[16,1,2048]{2,0,1:T(8,128)S(1)}, f32[16,1,2048]{2,0,1:T(8,128)S(1)}, u32[]{:S(2)}, u32[]{:S(2)}) collective-permute-start(f32[16,1,2048]{2,0,1:T(8,128)S(1)} %get-tuple-element.48), channel_id=1, source_target_pairs={{1,0},{3,2},{5,4},{7,6},{9,8},{11,10},{13,12},{15,14},{17,16},{19,... | collective-permute-start | bytes 393224 | tf_op jit(solution)/shard_map/ppermute | solution.py:60
  184.7 4.5 %collective-permute-start.21 = (f32[1,4,2048]{2,0,1:T(1,128)S(1)}, f32[1,4,2048]{2,0,1:T(1,128)S(1)}, u32[]{:S(2)}, u32[]{:S(2)}) collective-permute-start(f32[1,4,2048]{2,0,1:T(1,128)S(1)} %get-tuple-element.44), channel_id=1, source_target_pairs={{2,0},{4,2},{6,4},{8,6},{10,8},{12,10},{14,12},{16,14},{18,16},{20... | collective-permute-start | bytes 98312 | tf_op jit(solution)/shard_map/ppermute | solution.py:60
  (182 shorter events, 74.4 us)
Async XLA Ops:
  2.2 55.9 %collective-permute-start.2 = (f32[16,1,2048]{2,0,1:T(8,128)S(1)}, f32[16,1,2048]{2,0,1:T(8,128)}, u32[]{:S(2)}, u32[]{:S(2)}) collective-permute-start(f32[16,1,2048]{2,0,1:T(8,128)S(1)} %copy.139), channel_id=1, source_target_pairs={{0,1},{2,3},{4,5},{6,7},{8,9},{10,11},{12,13},{14,15},{16,17},{18,... | collective-permute-start | bytes 393224 | tf_op jit(solution)/shard_map/ppermute | solution.py:60
  4.2 53.9 %collective-permute-start.3 = (f32[16,1,2048]{2,0,1:T(8,128)}, f32[16,1,2048]{2,0,1:T(8,128)}, u32[]{:S(2)}, u32[]{:S(2)}) collective-permute-start(f32[16,1,2048]{2,0,1:T(8,128)} %copy.140), channel_id=1, source_target_pairs={{1,0},{3,2},{5,4},{7,6},{9,8},{11,10},{13,12},{15,14},{17,16},{19,... | collective-permute-start | bytes 393224 | tf_op jit(solution)/shard_map/ppermute | solution.py:60
  11.5 46.6 %collective-permute-start = (f32[1,4,2048]{2,0,1:T(1,128)}, f32[1,4,2048]{2,0,1:T(1,128)S(1)}, u32[]{:S(2)}, u32[]{:S(2)}) collective-permute-start(f32[1,4,2048]{2,0,1:T(1,128)} %copy.100), channel_id=1, source_target_pairs={{0,2},{2,4},{4,6},{6,8},{8,10},{10,12},{12,14},{14,16},{16,18},{18... | collective-permute-start | bytes 98312 | tf_op jit(solution)/shard_map/ppermute | solution.py:60
  14.1 44.0 %collective-permute-start.1 = (f32[1,4,2048]{2,0,1:T(1,128)}, f32[1,4,2048]{2,0,1:T(1,128)}, u32[]{:S(2)}, u32[]{:S(2)}) collective-permute-start(f32[1,4,2048]{2,0,1:T(1,128)} %copy.103), channel_id=1, source_target_pairs={{2,0},{4,2},{6,4},{8,6},{10,8},{12,10},{14,12},{16,14},{18,16},{20... | collective-permute-start | bytes 98312 | tf_op jit(solution)/shard_map/ppermute | solution.py:60
  61.4 13.9 %collective-permute-start.6 = (f32[16,1,2048]{2,0,1:T(8,128)S(1)}, f32[16,1,2048]{2,0,1:T(8,128)S(1)}, u32[]{:S(2)}, u32[]{:S(2)}) collective-permute-start(f32[16,1,2048]{2,0,1:T(8,128)S(1)} %get-tuple-element.95), channel_id=1, source_target_pairs={{0,1},{2,3},{4,5},{6,7},{8,9},{10,11},{12,13},{14,15},{16,17},{18,... | collective-permute-start | bytes 393224 | tf_op jit(solution)/shard_map/ppermute | solution.py:60
  62.7 12.6 %collective-permute-start.7 = (f32[16,1,2048]{2,0,1:T(8,128)S(1)}, f32[16,1,2048]{2,0,1:T(8,128)S(1)}, u32[]{:S(2)}, u32[]{:S(2)}) collective-permute-start(f32[16,1,2048]{2,0,1:T(8,128)S(1)} %get-tuple-element.96), channel_id=1, source_target_pairs={{1,0},{3,2},{5,4},{7,6},{9,8},{11,10},{13,12},{15,14},{17,16},{19,... | collective-permute-start | bytes 393224 | tf_op jit(solution)/shard_map/ppermute | solution.py:60
  67.2 6.6 %collective-permute-start.4 = (f32[1,4,2048]{2,0,1:T(1,128)S(1)}, f32[1,4,2048]{2,0,1:T(1,128)S(1)}, u32[]{:S(2)}, u32[]{:S(2)}) collective-permute-start(f32[1,4,2048]{2,0,1:T(1,128)S(1)} %get-tuple-element.91), channel_id=1, source_target_pairs={{0,2},{2,4},{4,6},{6,8},{8,10},{10,12},{12,14},{14,16},{16,18},{18... | collective-permute-start | bytes 98312 | tf_op jit(solution)/shard_map/ppermute | solution.py:60
  69.2 6.1 %collective-permute-start.5 = (f32[1,4,2048]{2,0,1:T(1,128)S(1)}, f32[1,4,2048]{2,0,1:T(1,128)S(1)}, u32[]{:S(2)}, u32[]{:S(2)}) collective-permute-start(f32[1,4,2048]{2,0,1:T(1,128)S(1)} %get-tuple-element.92), channel_id=1, source_target_pairs={{2,0},{4,2},{6,4},{8,6},{10,8},{12,10},{14,12},{16,14},{18,16},{20... | collective-permute-start | bytes 98312 | tf_op jit(solution)/shard_map/ppermute | solution.py:60
  76.6 13.9 %collective-permute-start.10 = (f32[16,1,2048]{2,0,1:T(8,128)S(1)}, f32[16,1,2048]{2,0,1:T(8,128)S(1)}, u32[]{:S(2)}, u32[]{:S(2)}) collective-permute-start(f32[16,1,2048]{2,0,1:T(8,128)S(1)} %get-tuple-element.83), channel_id=1, source_target_pairs={{0,1},{2,3},{4,5},{6,7},{8,9},{10,11},{12,13},{14,15},{16,17},{18,... | collective-permute-start | bytes 393224 | tf_op jit(solution)/shard_map/ppermute | solution.py:60
  77.9 12.6 %collective-permute-start.11 = (f32[16,1,2048]{2,0,1:T(8,128)S(1)}, f32[16,1,2048]{2,0,1:T(8,128)S(1)}, u32[]{:S(2)}, u32[]{:S(2)}) collective-permute-start(f32[16,1,2048]{2,0,1:T(8,128)S(1)} %get-tuple-element.84), channel_id=1, source_target_pairs={{1,0},{3,2},{5,4},{7,6},{9,8},{11,10},{13,12},{15,14},{17,16},{19,... | collective-permute-start | bytes 393224 | tf_op jit(solution)/shard_map/ppermute | solution.py:60
  82.5 6.6 %collective-permute-start.8 = (f32[1,4,2048]{2,0,1:T(1,128)S(1)}, f32[1,4,2048]{2,0,1:T(1,128)S(1)}, u32[]{:S(2)}, u32[]{:S(2)}) collective-permute-start(f32[1,4,2048]{2,0,1:T(1,128)S(1)} %get-tuple-element.79), channel_id=1, source_target_pairs={{0,2},{2,4},{4,6},{6,8},{8,10},{10,12},{12,14},{14,16},{16,18},{18... | collective-permute-start | bytes 98312 | tf_op jit(solution)/shard_map/ppermute | solution.py:60
  84.4 6.1 %collective-permute-start.9 = (f32[1,4,2048]{2,0,1:T(1,128)S(1)}, f32[1,4,2048]{2,0,1:T(1,128)S(1)}, u32[]{:S(2)}, u32[]{:S(2)}) collective-permute-start(f32[1,4,2048]{2,0,1:T(1,128)S(1)} %get-tuple-element.80), channel_id=1, source_target_pairs={{2,0},{4,2},{6,4},{8,6},{10,8},{12,10},{14,12},{16,14},{18,16},{20... | collective-permute-start | bytes 98312 | tf_op jit(solution)/shard_map/ppermute | solution.py:60
  100.9 9.9 %all-to-all-start = ((f32[16,1,2048]{2,1,0:T(1,128)}), f32[16,1,2048]{2,1,0:T(1,128)S(1)}, u32[]{:S(2)}, u32[]{:S(2)}) async-start(f32[16,1,2048]{2,1,0:T(1,128)} %reshape.115), calls=%async_computation | async-start | bytes 262144 | tf_op jit(solution)/shard_map/all_to_all | solution.py:113
  130.7 19.6 %all-to-all-start.1 = ((f32[16,1,2048]{2,1,0:T(1,128)}), f32[16,1,2048]{2,1,0:T(1,128)S(1)}, u32[]{:S(2)}, u32[]{:S(2)}) async-start(f32[16,1,2048]{2,1,0:T(1,128)} %reshape.117), calls=%async_computation.1 | async-start | bytes 262144 | tf_op jit(solution)/shard_map/all_to_all | solution.py:128
  136.0 23.4 %collective-permute-start.14 = (f32[16,1,2048]{2,0,1:T(8,128)}, f32[16,1,2048]{2,0,1:T(8,128)}, u32[]{:S(2)}, u32[]{:S(2)}) collective-permute-start(f32[16,1,2048]{2,0,1:T(8,128)} %get-tuple-element.71), channel_id=1, source_target_pairs={{0,1},{2,3},{4,5},{6,7},{8,9},{10,11},{12,13},{14,15},{16,17},{18,... | collective-permute-start | bytes 393224 | tf_op jit(solution)/shard_map/ppermute | solution.py:60
  137.3 22.1 %collective-permute-start.15 = (f32[16,1,2048]{2,0,1:T(8,128)}, f32[16,1,2048]{2,0,1:T(8,128)}, u32[]{:S(2)}, u32[]{:S(2)}) collective-permute-start(f32[16,1,2048]{2,0,1:T(8,128)} %get-tuple-element.72), channel_id=1, source_target_pairs={{1,0},{3,2},{5,4},{7,6},{9,8},{11,10},{13,12},{15,14},{17,16},{19,... | collective-permute-start | bytes 393224 | tf_op jit(solution)/shard_map/ppermute | solution.py:60
  143.2 16.2 %collective-permute-start.12 = (f32[1,4,2048]{2,0,1:T(1,128)}, f32[1,4,2048]{2,0,1:T(1,128)}, u32[]{:S(2)}, u32[]{:S(2)}) collective-permute-start(f32[1,4,2048]{2,0,1:T(1,128)} %get-tuple-element.67), channel_id=1, source_target_pairs={{0,2},{2,4},{4,6},{6,8},{8,10},{10,12},{12,14},{14,16},{16,18},{18... | collective-permute-start | bytes 98312 | tf_op jit(solution)/shard_map/ppermute | solution.py:60
  145.1 14.3 %collective-permute-start.13 = (f32[1,4,2048]{2,0,1:T(1,128)}, f32[1,4,2048]{2,0,1:T(1,128)}, u32[]{:S(2)}, u32[]{:S(2)}) collective-permute-start(f32[1,4,2048]{2,0,1:T(1,128)} %get-tuple-element.68), channel_id=1, source_target_pairs={{2,0},{4,2},{6,4},{8,6},{10,8},{12,10},{14,12},{16,14},{18,16},{20... | collective-permute-start | bytes 98312 | tf_op jit(solution)/shard_map/ppermute | solution.py:60
  161.8 13.9 %collective-permute-start.18 = (f32[16,1,2048]{2,0,1:T(8,128)S(1)}, f32[16,1,2048]{2,0,1:T(8,128)S(1)}, u32[]{:S(2)}, u32[]{:S(2)}) collective-permute-start(f32[16,1,2048]{2,0,1:T(8,128)S(1)} %get-tuple-element.59), channel_id=1, source_target_pairs={{0,1},{2,3},{4,5},{6,7},{8,9},{10,11},{12,13},{14,15},{16,17},{18,... | collective-permute-start | bytes 393224 | tf_op jit(solution)/shard_map/ppermute | solution.py:60
  163.1 12.6 %collective-permute-start.19 = (f32[16,1,2048]{2,0,1:T(8,128)S(1)}, f32[16,1,2048]{2,0,1:T(8,128)S(1)}, u32[]{:S(2)}, u32[]{:S(2)}) collective-permute-start(f32[16,1,2048]{2,0,1:T(8,128)S(1)} %get-tuple-element.60), channel_id=1, source_target_pairs={{1,0},{3,2},{5,4},{7,6},{9,8},{11,10},{13,12},{15,14},{17,16},{19,... | collective-permute-start | bytes 393224 | tf_op jit(solution)/shard_map/ppermute | solution.py:60
  167.7 7.7 %collective-permute-start.16 = (f32[1,4,2048]{2,0,1:T(1,128)S(1)}, f32[1,4,2048]{2,0,1:T(1,128)S(1)}, u32[]{:S(2)}, u32[]{:S(2)}) collective-permute-start(f32[1,4,2048]{2,0,1:T(1,128)S(1)} %get-tuple-element.55), channel_id=1, source_target_pairs={{0,2},{2,4},{4,6},{6,8},{8,10},{10,12},{12,14},{14,16},{16,18},{18... | collective-permute-start | bytes 98312 | tf_op jit(solution)/shard_map/ppermute | solution.py:60
  176.9 13.9 %collective-permute-start.22 = (f32[16,1,2048]{2,0,1:T(8,128)S(1)}, f32[16,1,2048]{2,0,1:T(8,128)S(1)}, u32[]{:S(2)}, u32[]{:S(2)}) collective-permute-start(f32[16,1,2048]{2,0,1:T(8,128)S(1)} %get-tuple-element.47), channel_id=1, source_target_pairs={{0,1},{2,3},{4,5},{6,7},{8,9},{10,11},{12,13},{14,15},{16,17},{18,... | collective-permute-start | bytes 393224 | tf_op jit(solution)/shard_map/ppermute | solution.py:60
  178.2 12.6 %collective-permute-start.23 = (f32[16,1,2048]{2,0,1:T(8,128)S(1)}, f32[16,1,2048]{2,0,1:T(8,128)S(1)}, u32[]{:S(2)}, u32[]{:S(2)}) collective-permute-start(f32[16,1,2048]{2,0,1:T(8,128)S(1)} %get-tuple-element.48), channel_id=1, source_target_pairs={{1,0},{3,2},{5,4},{7,6},{9,8},{11,10},{13,12},{15,14},{17,16},{19,... | collective-permute-start | bytes 393224 | tf_op jit(solution)/shard_map/ppermute | solution.py:60
  182.7 6.6 %collective-permute-start.20 = (f32[1,4,2048]{2,0,1:T(1,128)S(1)}, f32[1,4,2048]{2,0,1:T(1,128)S(1)}, u32[]{:S(2)}, u32[]{:S(2)}) collective-permute-start(f32[1,4,2048]{2,0,1:T(1,128)S(1)} %get-tuple-element.43), channel_id=1, source_target_pairs={{0,2},{2,4},{4,6},{6,8},{8,10},{10,12},{12,14},{14,16},{16,18},{18... | collective-permute-start | bytes 98312 | tf_op jit(solution)/shard_map/ppermute | solution.py:60
  (34 other events, 228.8 us)

commit v2 on v1

--- a/solution.py
+++ b/solution.py
@@ -2,6 +2,8 @@
 import jax.numpy as jnp
 import numpy as np
 from jax import lax
+from jax.experimental import pallas as pl
+from jax.experimental.pallas import tpu as pltpu
 from jax.sharding import PartitionSpec as P
 
 MODES = 256
@@ -51,31 +53,128 @@
     return basis, weighted
 
 
-def neighbours(x, axis, dim):
-    devices, length = (lax.axis_size(axis), x.shape[dim])
-    up = [(i, i + 1) for i in range(devices - 1)]
-    down = [(j, i) for i, j in up]
-    last = lax.slice_in_dim(x, length - 1, length, axis=dim)
-    first = lax.slice_in_dim(x, 0, 1, axis=dim)
-    return lax.ppermute(last, axis, up), lax.ppermute(first, axis, down)
-
-
-def sweep(field, memory, source, stiff, decay):
-    beside = jnp.roll(field, 1, axis=2) + jnp.roll(field, -1, axis=2)
-    for axis, dim in (("lat", 0), ("rad", 1)):
-        length = field.shape[dim]
-        before, after = neighbours(field, axis, dim)
-        beside = beside + jnp.concatenate(
-            [before, lax.slice_in_dim(field, 0, length - 1, axis=dim)], axis=dim
+def sweeps_kernel(steps, gather, *refs):
+    if gather:
+        f_ref, m_ref, s_ref, stiff_ref, decay_ref, g_ref, f_out, m_out, g_out, *refs = refs
+        f_buf, face, lat_in, rad_in, send, recv, g_in, g_send, g_recv = refs
+    else:
+        f_ref, m_ref, s_ref, stiff_ref, decay_ref, f_out, m_out, *refs = refs
+        f_buf, face, lat_in, rad_in, send, recv = refs
+    layers, rows, nlon = f_ref.shape
+    lat_n, rad_n = lax.axis_size("lat"), lax.axis_size("rad")
+    lat, rad = lax.axis_index("lat"), lax.axis_index("rad")
+    north = (lax.rem(lat + lat_n - 1, lat_n), rad)
+    south = (lax.rem(lat + 1, lat_n), rad)
+    below = (lat, lax.rem(rad + rad_n - 1, rad_n))
+    above = (lat, lax.rem(rad + 1, rad_n))
+    if gather:
+        peers = [(lax.rem(lat + d, lat_n), rad) for d in range(1, lat_n)] + [below, above]
+    else:
+        peers = [north, south, below, above]
+    barrier = pltpu.get_barrier_semaphore()
+    for peer in peers:
+        pl.semaphore_signal(barrier, inc=1, device_id=peer, device_id_type=pl.DeviceIdType.MESH)
+    pl.semaphore_wait(barrier, len(peers))
+
+    def remote(src, dst, send_sem, recv_sem, peer):
+        copy = pltpu.make_async_remote_copy(
+            src_ref=src, dst_ref=dst, send_sem=send_sem, recv_sem=recv_sem,
+            device_id=peer, device_id_type=pl.DeviceIdType.MESH,
         )
-        beside = beside + jnp.concatenate(
-            [lax.slice_in_dim(field, 1, length, axis=dim), after], axis=dim
-        )
-    diagonal = 6.0 + kappa_shift
-    update = relax_factor * (
-        (source - memory) * (1.0 / (stiff * diagonal)) - field + beside * (1.0 / diagonal)
-    )
-    return (field + update, decay * memory + stiff * update)
+        copy.start()
+        return copy
+
+    weight = relax_factor / (6.0 + kappa_shift)
+    w_north = jnp.where(lat > 0, weight, 0.0)
+    w_south = jnp.where(lat < lat_n - 1, weight, 0.0)
+    w_below = jnp.where(rad > 0, weight, 0.0)
+    w_above = jnp.where(rad < rad_n - 1, weight, 0.0)
+    row = lax.broadcasted_iota(jnp.int32, (rows, nlon), 0)
+    gathered = []
+    for step in range(steps):
+        old = f_ref if step == 0 else f_buf.at[step - 1]
+        new = f_out if step == steps - 1 else f_buf.at[step]
+        old_m = m_ref if step == 0 else m_out
+        for r in range(layers):
+            face[step, 0, r : r + 1, :] = old[r, 0:1, :]
+            face[step, 1, r : r + 1, :] = old[r, rows - 1 : rows, :]
+        copies = [
+            remote(old.at[0], rad_in.at[step, 1], send.at[step, 0], recv.at[step, 0], below),
+            remote(old.at[layers - 1], rad_in.at[step, 0], send.at[step, 1], recv.at[step, 1], above),
+            remote(face.at[step, 0], lat_in.at[step, 1], send.at[step, 2], recv.at[step, 2], north),
+            remote(face.at[step, 1], lat_in.at[step, 0], send.at[step, 3], recv.at[step, 3], south),
+        ]
+        if gather and step == 0:
+            gathered = [
+                remote(g_ref, g_in.at[lat], g_send.at[d], g_recv.at[d], peers[d - 1])
+                for d in range(1, lat_n)
+            ]
+        for r in range(layers):
+            f, m = old[r], old_m[r]
+            beside = pltpu.roll(f, 1, 1) + pltpu.roll(f, nlon - 1, 1)
+            beside += jnp.where(row == 0, 0.0, pltpu.roll(f, 1, 0))
+            beside += jnp.where(row == rows - 1, 0.0, pltpu.roll(f, rows - 1, 0))
+            if r > 0:
+                beside += old[r - 1]
+            if r < layers - 1:
+                beside += old[r + 1]
+            stiff = stiff_ref[r]
+            update = (s_ref[r] - m) * (weight / stiff) - relax_factor * f + weight * beside
+            new[r] = f + update
+            m_out[r] = decay_ref[r] * m + stiff * update
+        for copy in copies:
+            copy.wait()
+        for r, slot, w in ((0, 0, w_below), (layers - 1, 1, w_above)):
+            extra = w * rad_in[step, slot]
+            new[r] += extra
+            m_out[r] += stiff_ref[r] * extra
+        for r in range(layers):
+            for j, slot, w in ((0, 0, w_north), (rows - 1, 1, w_south)):
+                extra = w * lat_in[step, slot, r : r + 1, :]
+                new[r, j : j + 1, :] += extra
+                m_out[r, j : j + 1, :] += stiff_ref[r, j : j + 1, :] * extra
+    if gather:
+        for copy in gathered:
+            copy.wait()
+        g_in[lat] = g_ref[...]
+        g_out[...] = g_in[...]
+
+
+def sweeps(steps, field, memory, source, stiff, decay, gravity=None):
+    gather = gravity is not None
+    layers, rows, nlon = field.shape
+    block = jax.ShapeDtypeStruct(field.shape, jnp.float32)
+    operands, out = [field, memory, source, stiff, decay], [block, block]
+    dma, f32 = pltpu.SemaphoreType.DMA, jnp.float32
+    scratch = [
+        pltpu.VMEM((steps - 1, layers, rows, nlon), f32),
+        pltpu.VMEM((steps, 2, layers, nlon), f32),
+        pltpu.VMEM((steps, 2, layers, nlon), f32),
+        pltpu.VMEM((steps, 2, rows, nlon), f32),
+        dma((steps, 4)),
+        dma((steps, 4)),
+    ]
+    if gather:
+        lat_n = lax.axis_size("lat")
+        every = (lat_n,) + gravity.shape
+        operands.append(gravity)
+        out.append(jax.ShapeDtypeStruct(every, f32))
+        scratch += [pltpu.VMEM(every, f32), dma((lat_n,)), dma((lat_n,))]
+    vmem = pl.BlockSpec(memory_space=pltpu.VMEM)
+
+    def kernel(*refs):
+        sweeps_kernel(steps, gather, *refs)
+
+    return pl.pallas_call(
+        kernel,
+        out_shape=out,
+        in_specs=[vmem] * len(operands),
+        out_specs=[vmem] * len(out),
+        scratch_shapes=scratch,
+        compiler_params=pltpu.CompilerParams(
+            collective_id=0 if gather else 1, has_side_effects=True
+        ),
+    )(*operands)
 
 
 def per_device(
@@ -90,14 +189,13 @@
     degrees = gravity_kernel.shape[0] * lat_count
     cols = 2 * MODES
     columns = cols // lat_count
-    kernel_every = lax.all_gather(gravity_kernel, "lat", axis=0, tiled=True)
-    stiff = lookup(material, mu_table)[:, :, None]
-    decay = lookup(material, decay_table)[:, :, None]
-    contrast = lookup(material, contrast_table)[:, :, None]
+    stiff = lookup(material.T, mu_table)[:, :, None]
+    decay = lookup(material.T, decay_table)[:, :, None]
+    contrast = lookup(material.T, contrast_table)[:, :, None]
     layer_pos = (rad_index * r_dev + jnp.arange(r_dev, dtype=jnp.int32) + 1).astype(
         jnp.float32
     ) / total_rad
-    source = load_scale * ice_class.astype(jnp.float32)[:, None, :] * layer_pos[None, :, None]
+    source = load_scale * ice_class.astype(jnp.float32)[None, :, :] * layer_pos[:, None, None]
     basis, weighted = legendre(total_lat, degrees)
     projection = jnp.asarray(
         np.concatenate([weighted, np.ones((8, total_lat))]).astype(np.float32)
@@ -105,13 +203,20 @@
     weight_sum = jnp.asarray(weighted.sum(axis=1).astype(np.float32))
     basis = jnp.asarray(basis.T.astype(np.float32))
     table = fourier_table(nlon, MODES)
-    field, mem = (displacement, memory)
-    for step in range(3):
-        field, mem = sweep(field, mem, source, stiff, decay)
+    field, mem, kernel_every = sweeps(
+        3,
+        displacement.transpose(1, 0, 2),
+        memory.transpose(1, 0, 2),
+        source,
+        stiff,
+        decay,
+        gravity_kernel.reshape(gravity_kernel.shape[0], -1),
+    )
+    kernel_every = kernel_every.reshape((degrees,) + gravity_kernel.shape[1:])
     rho = contrast * field
     spectra = jnp.dot(rho.reshape(lat_dev * r_dev, nlon), table, precision=HIGH)
     spread = lax.all_to_all(
-        spectra.reshape(lat_dev, r_dev, cols), "lat", split_axis=2, concat_axis=0, tiled=True
+        spectra.reshape(r_dev, lat_dev, cols).transpose(1, 0, 2), "lat", split_axis=2, concat_axis=0, tiled=True
     )
     coef_cols = jnp.dot(
         projection, spread.reshape(total_lat, r_dev * columns), precision=HIGH
@@ -127,12 +232,11 @@
     ).reshape(total_lat, r_dev, columns)
     synth = lax.all_to_all(synth_cols, "lat", split_axis=0, concat_axis=2, tiled=True)
     potential = lax.dot_general(
-        synth.reshape(lat_dev * r_dev, cols), table, (((1,), (1,)), ((), ())), precision=HIGH
-    ).reshape(lat_dev, r_dev, nlon)
+        synth.transpose(1, 0, 2).reshape(r_dev * lat_dev, cols), table, (((1,), (1,)), ((), ())), precision=HIGH
+    ).reshape(r_dev, lat_dev, nlon)
     loaded = source + coupling * potential
-    for step in range(3):
-        field, mem = sweep(field, mem, loaded, stiff, decay)
-    return (field, mem, potential)
+    field, mem = sweeps(3, field, mem, loaded, stiff, decay)
+    return tuple(x.transpose(1, 0, 2) for x in (field, mem, potential))
 
 
 def solution(mesh):

time: 197 us -> 118 us (0.60)
  the two profiles are of different devices: /device:TPU:10 before, /device:TPU:0 now
where the time goes in v2:
time: 118 us; the launch traced here: 117 us
  Pallas kernels  54.2 us (46%)
  local copies, waits for them, and re-layouts  18.9 us (16%)
  blocking collectives  17.7 us (15%)
  matrix products  8.31 us (7%)
  waiting for transfers between devices  6.92 us (6%)
  other arithmetic  6.74 us (6%)
  starting transfers between devices  3.51 us (3%)
    pallas_call x2, Pallas kernels, sweeps(): pl.pallas_call(kernel, out_shape=out, in_specs=[vmem] * len(operands), ou...  54.2 us
    all_to_all x1, blocking collectives, per_device(): lax.all_to_all(synth_cols, 'lat', split_axis=0, concat_axis=2, tiled=True)  10.9 us
    unnamed x25, local copies, waits for them, and re-layouts  8.34 us
    all_to_all x1, waiting for transfers between devices, per_device(): lax.all_to_all(spectra.reshape(r_dev, lat_dev, cols).transpose(1, 0, 2),...  6.92 us
    all_gather x1, blocking collectives, per_device(): coef_all = lax.all_gather(coef_cols, 'rad', axis=1, tiled=True)  6.77 us
    dot_general x1, matrix products, per_device(): lax.dot_general(synth.transpose(1, 0, 2).reshape(r_dev * lat_dev, cols),...  4.43 us
    all_to_all x1, starting transfers between devices, per_device(): lax.all_to_all(spectra.reshape(r_dev, lat_dev, cols).transpose(1, 0, 2),...  3.51 us
    dot_general x1, matrix products, per_device(): spectra = jnp.dot(rho.reshape(lat_dev * r_dev, nlon), table, precision=HIGH)  3.22 us
  transfers between devices with their start and end apart: 1, of which 1 were waited for; matrix products, arithmetic and copies ran while one was open for 1% of the time, Pallas kernels for 0%

profile of v2, /device:TPU:0, one launch (start us, length us, event | category | flops | bytes accessed | tf_op | source)
XLA Modules:
  0.0 117.2 jit_solution(7253244172800817282)
XLA Ops:
  0.7 1.5 %copy.69.refs_5_ = f32[16,32]{1,0:T(8,128)} copy(f32[16,32]{0,1:T(8,128)} %bitcast.62) | data formatting | bytes 4096 | tf_op jit(solution)/shard_map/reshape | solution.py:213
  2.2 0.8 select_reduce_fusion
  4.4 0.9 convert_multiply_fusion
  5.3 0.9 broadcast_multiply_fusion.refs_2_
  6.2 2.8 %copy_bitcast_fusion = (f32[4,16,2048]{2,1,0:T(8,128)}, f32[4,16,2048]{2,1,0:T(8,128)}) fusion(f32[16,4,2048]{2,1,0:T(4,128)} %param.16, f32[16,4,2048]{2,1,0:T(4,128)} %param.15), kind=kLoop, calls=%fused_computation.7 | loop fusion | bytes 2097152 | tf_op jit(solution)/shard_map/transpose | solution.py:209
  9.0 1.9 %multiply_subtract_fusion = (f32[16,128,256]{2,1,0:T(8,128)S(1)}, f32[16,128,256]{2,1,0:T(8,128)}) fusion(f32[128,256]{1,0:T(8,128)S(1)} %copy-done.2, f32[16,256]{1,0:T(8,128)S(1)} %copy-done.6, f32[128,256]{1,0:T(8,128)S(1)} %copy-done.3, f32[16,256]{1,0:T(8,128)S(1)} %copy-done.7), kind=kLoop, calls=%fused_computation.4 | loop fusion | flops 3145728 | bytes 4489216 | tf_op jit(solution)/shard_map/sub | solution.py:39
  10.9 31.1 %shard_map.166 = (f32[4,16,2048]{2,1,0:T(8,128)}, f32[4,16,2048]{2,1,0:T(8,128)}, f32[16,16,32]{2,1,0:T(8,128)}) custom-call(f32[4,16,2048]{2,1,0:T(8,128)} %get-tuple-element.41.refs_0_, f32[4,16,2048]{2,1,0:T(8,128)} %get-tuple-element.40.refs_1_, f32[4,16,2048]{2,1,0:T(8,128)} %broadcast_multiply_fusion.refs_2_, f32[4,16,1]{2,1,0:T(8,128)} %copy.67.refs_3_, ...), custom_call_target="tpu_custom_call" | custom-call | tf_op jit(solution)/shard_map/pallas_call | solution.py:168
  42.0 3.2 %fusion.2 = f32[16,4,512]{2,0,1:T(8,128)S(1)} fusion(f32[2048,256]{1,0:T(8,128)} %bitcast.50, f32[2048,256]{1,0:T(8,128)S(1)} %bitcast.48, f32[4,16,2048]{2,1,0:T(8,128)} %get-tuple-element.12.refs_0_, f32[4,16]{1,0:T(4,128)S(1)} %get-tuple-element.33), kind=kOutput, calls=%fused_computation.5 | convolution fusion | flops 403832832 | bytes 4849920 | tf_op jit(solution)/shard_map/dot_general | solution.py:217
  45.7 1.5 %reshape.110 = f32[16,1,2048]{2,1,0:T(1,128)} reshape(f32[512,4,16]{2,1,0:T(4,128)S(1)} %bitcast.52) | data formatting | bytes 262144
  47.1 3.5 %all-to-all-start = ((f32[16,1,2048]{2,1,0:T(1,128)}), f32[16,1,2048]{2,1,0:T(1,128)S(1)}, u32[]{:S(2)}, u32[]{:S(2)}) async-start(f32[16,1,2048]{2,1,0:T(1,128)} %reshape.110), calls=%async_computation | async-start | bytes 262144 | tf_op jit(solution)/shard_map/all_to_all | solution.py:218
  50.8 0.8 mul.159
  51.6 6.9 %all-to-all-done = f32[16,1,2048]{2,1,0:T(1,128)S(1)} async-done(((f32[16,1,2048]{2,1,0:T(1,128)}), f32[16,1,2048]{2,1,0:T(1,128)S(1)}, u32[]{:S(2)}, u32[]{:S(2)}) %all-to-all-start) | async-done | bytes 131104 | tf_op jit(solution)/shard_map/all_to_all | solution.py:218
  59.0 0.9 reduce.1
  60.0 0.7 reshape.111
  60.8 1.1 copy.72
  61.9 1.3 %reshape.105 = f32[256,128]{1,0:T(8,128)S(1)} reshape(f32[16,16,4,32]{3,2,1,0:T(4,128)} %bitcast.54) | data formatting | bytes 262144 | tf_op jit(solution)/shard_map/reshape | solution.py:222
  63.6 6.8 %all_gather.3 = f32[264,8,32]{0,2,1:T(8,128)S(1)} all-gather(f32[264,4,32]{0,2,1:T(8,128)S(1)} %bitcast.57), channel_id=1, replica_groups=mesh['lat'=16,'rad'=2] {'rad'}, dimensions={1}, use_global_device_ids=true | all-gather | bytes 405504 | tf_op jit(solution)/shard_map/all_gather | solution.py:224
  71.6 10.9 %all_to_all.33 = f32[16,1,2048]{2,1,0:T(1,128)S(1)} all-to-all(f32[16,1,2048]{2,1,0:T(1,128)S(1)} %reshape.112), channel_id=1, replica_groups=mesh['lat'=16,'rad'=2] {'lat'}, dimensions={0} | all-to-all | bytes 262144 | tf_op jit(solution)/shard_map/all_to_all | solution.py:233
  82.5 0.9 reduce.2
  84.2 4.4 %multiply_add_fusion.1 = (f32[4,16,2048]{2,1,0:T(8,128)}, f32[4,16,2048]{2,1,0:T(8,128)S(1)}) fusion(f32[4]{0:T(128)S(1)} %convert_multiply_fusion.1, f32[16,2048]{1,0:T(8,128)S(1)} %convert_multiply_fusion, f32[2048,256]{1,0:T(8,128)} %bitcast.51, f32[2048,256]{1,0:T(8,128)S(1)} %bitcast.49, f32[16,4,512]{2,0,1:T(8,128)S(1)} %all_to_all.30), kind=kOutput, calls=%fused_computation.9 | convolution fusion | flops 404094976 | bytes 5505040 | tf_op jit(solution)/shard_map/dot_general | solution.py:234
  88.6 23.1 %shard_map.167 = (f32[4,16,2048]{2,1,0:T(8,128)}, f32[4,16,2048]{2,1,0:T(8,128)}) custom-call(f32[4,16,2048]{2,1,0:T(8,128)} %get-tuple-element.12.refs_0_, f32[4,16,2048]{2,1,0:T(8,128)} %get-tuple-element.13.refs_1_, f32[4,16,2048]{2,1,0:T(8,128)} %get-tuple-element.38.refs_2_, f32[4,16,1]{2,1,0:T(8,128)} %copy.67.refs_3_, f32[4,16,1]{2,1,0:T(8,128)} %copy.68.refs_4_), custom_call_target="tpu_custom_call" | custom-call | tf_op jit(solution)/shard_map/pallas_call | solution.py:168
  111.7 2.2 %copy.79 = f32[16,4,2048]{2,1,0:T(4,128)} copy(f32[16,4,2048]{2,0,1:T(8,128)} %bitcast.59) | data formatting | bytes 1048576
  113.9 2.2 %copy.80 = f32[16,4,2048]{2,1,0:T(4,128)} copy(f32[16,4,2048]{2,0,1:T(8,128)} %bitcast.58) | data formatting | bytes 1048576
  116.1 1.1 copy.81
  (37 shorter events, 4.8 us)
Async XLA Ops:
  0.6 8.3 %copy-start.2 = (f32[128,256]{1,0:T(8,128)S(1)}, f32[128,256]{1,0:T(8,128)}, u32[]{:S(2)}) copy-start(f32[128,256]{1,0:T(8,128)} %constant.51.clone) | copy-start | bytes 393220
  0.6 8.3 %copy-start.3 = (f32[128,256]{1,0:T(8,128)S(1)}, f32[128,256]{1,0:T(8,128)}, u32[]{:S(2)}) copy-start(f32[128,256]{1,0:T(8,128)} %constant.50.clone) | copy-start | bytes 393220
  0.7 8.3 %copy-start.6 = (f32[16,256]{1,0:T(8,128)S(1)}, f32[16,256]{1,0:T(8,128)}, u32[]{:S(2)}) copy-start(f32[16,256]{1,0:T(8,128)} %constant.49.clone) | copy-start | bytes 49156
  0.7 8.3 %copy-start.7 = (f32[16,256]{1,0:T(8,128)S(1)}, f32[16,256]{1,0:T(8,128)}, u32[]{:S(2)}) copy-start(f32[16,256]{1,0:T(8,128)} %constant.48.clone) | copy-start | bytes 49156
  45.2 5.4 %copy-start.4 = (f32[16,16,32]{2,1,0:T(8,128)S(1)}, f32[16,16,32]{2,1,0:T(8,128)}, u32[]{:S(2)}) copy-start(f32[16,16,32]{2,1,0:T(8,128)} %get-tuple-element.14) | copy-start | bytes 98308
  47.1 11.4 %all-to-all-start = ((f32[16,1,2048]{2,1,0:T(1,128)}), f32[16,1,2048]{2,1,0:T(1,128)S(1)}, u32[]{:S(2)}, u32[]{:S(2)}) async-start(f32[16,1,2048]{2,1,0:T(1,128)} %reshape.110), calls=%async_computation | async-start | bytes 262144 | tf_op jit(solution)/shard_map/all_to_all | solution.py:218
  60.0 10.5 %copy-start.8 = (f32[256]{0:T(256)S(1)}, f32[256]{0:T(256)}, u32[]{:S(2)}) copy-start(f32[256]{0:T(256)} %constant.46.clone) | copy-start | bytes 3076
  60.7 2.5 %copy-start = (f32[264,256]{1,0:T(8,128)S(1)}, f32[264,256]{1,0:T(8,128)}, u32[]{:S(2)}) copy-start(f32[264,256]{1,0:T(8,128)} %constant.45.clone) | copy-start | bytes 811012
  61.9 8.7 %copy-start.5 = (f32[256,4,8]{0,2,1:T(8,128)S(1)}, f32[256,4,8]{0,2,1:T(8,128)}, u32[]{:S(2)}) copy-start(f32[256,4,8]{0,2,1:T(8,128)} %mul.159) | copy-start | bytes 98308
  61.9 8.8 %copy-start.1 = (f32[256,256]{1,0:T(8,128)S(1)}, f32[256,256]{1,0:T(8,128)}, u32[]{:S(2)}) copy-start(f32[256,256]{1,0:T(8,128)} %constant.47.clone) | copy-start | bytes 786436
